TPU v7x, 256 devices: a whole 4x4x8 slice. The times are simulated.
256 devices in a mesh: gx: 32 (over x, z), gy: 8 (over y, core).
Axes of the slice: x: 4, y: 4, z: 8, core: 2. Of those that a mesh axis runs over, the one named last changes fastest.
Arguments:
- spheres: float32 [13, 8, 256, 128], P(None, 'gy', 'gx')
- new_home: int32 [8, 256], P('gy', 'gx'), may hold values from 0 to 255, as said below
- ghost_list: int32 [8, 64], P('gy', 'gx'), may hold values from 0 to 7, as said below
- tile_pairs: int32 [8, 8192, 2], P('gy', 'gx'), may hold values from 0 to 25, as said below
- tile_count: int32 [8, 32], P('gy', 'gx'), may hold values from 24 to 256
Outputs:
- updated: float32 [13, 8, 256, 128], P(None, 'gy', 'gx')
Inputs may be any that keep to these rules, and one draw needn't show every extreme that they name: Within each row new_home is a permutation of the row's slots; a block in slot b moves to the device 0 to 3 slabs ahead along gx, cyclically; some block moves exactly 3 slabs. `ghost_list`: the 2 entries of one device are distinct. `tile_pairs`: column 0 is a local block; column 1 is a pool entry below 16 or from 18 on; every such pool entry appears in a valid tile of every device.
All inputs are finite; a program needn't handle non-finite values.
Results may differ from a plain program's by a relative error of at most 0.0003.
Values sent between devices are 32-bit elements; how exact they have to be, the bound alone decides.
No kernel may reach another device: no remote copies, remote signals or barrier semaphores. Data moves between devices by JAX's collectives and lax.ppermute only.
A program may use at most 64 MiB of HBM per device.

v0:
```python
import jax
import jax.numpy as jnp
from jax import lax
from jax.experimental import pallas as pl
from jax.experimental.pallas import tpu as pltpu
from jax.sharding import PartitionSpec as P


DT = 0.01
DENSITY = 240.0
SC = 20.0
NB = 8
NP = 26
NT = NB * NP
U = 8
LAG = 2

f32 = jnp.float32
bf16 = jnp.bfloat16
i32 = jnp.int32


def passed_along(x, axis, by):
    peers = lax.axis_size(axis)
    return lax.ppermute(x, axis, [(i, (i + by) % peers) for i in range(peers)])


def embed_kernel(home_ref, lent_ref, x_ref, out, slots):
    out[0:13] = x_ref[...]
    row = lax.broadcasted_iota(i32, (NB, 128), 0)
    home = jnp.zeros((NB, 128), i32)
    for b in range(NB):
        home = jnp.where(row == b, home_ref[0, b], home)
    out[13] = home.astype(f32)
    slots[...] = jnp.where(row == 0, lent_ref[0, 0], lent_ref[0, 1]).astype(f32)


def pick(x, slots, out, at):
    row = lax.broadcasted_iota(i32, (NB, 128), 0).astype(f32)
    for q in range(2):
        chosen = row == jnp.broadcast_to(slots[q : q + 1, :], (NB, 128))
        for c in range(13):
            out[at + 16 * q + c : at + 16 * q + c + 1, :] = jnp.sum(
                jnp.where(chosen, x[c], 0.0), 0, keepdims=True
            )
        out[at + 16 * q + 13 : at + 16 * q + 16, :] = jnp.zeros((3, 128), f32)


def sort_kernel(mine, past, slots, next_slots, keep, ship, lent, lent_next):
    me = lax.axis_index("gx").astype(i32)
    row = lax.broadcasted_iota(i32, (NB, 128), 0)
    here = (me * NB + row).astype(f32)
    there = (((me + 1) & 31) * NB + row).astype(f32)
    held = []
    for ref in (mine, past):
        for t in range(NB):
            home = ref[13] if t == 0 else pltpu.roll(ref[13], t, 0)
            held.append((ref, t, home == here, home == there))
    stays, goes = [], []
    for c in range(13):
        stay = jnp.zeros((NB, 128), f32)
        go = jnp.zeros((NB, 128), f32)
        for ref, t, is_here, is_there in held:
            x = ref[c] if t == 0 else pltpu.roll(ref[c], t, 0)
            stay = jnp.where(is_here, x, stay)
            go = jnp.where(is_there, x, go)
        stays.append(stay)
        goes.append(go)
    for x in (stays, goes):
        for c in range(3):
            x[c] = x[c] + DT * x[3 + c] + (0.5 * DT * DT) * x[9 + c]
    for c in range(13):
        keep[c] = stays[c]
        ship[8 * c : 8 * c + 8, :] = goes[c]
    pick(stays, slots, lent, 0)
    ship[104:136, :] = lent[...]
    pick(goes, next_slots, lent_next, 0)


def join_kernel(keep, came, far, fore, lent_next, slots, drifted, line):
    x = [keep[c] + came[8 * c : 8 * c + 8, :] for c in range(13)]
    for c in range(13):
        drifted[c] = x[c]
    line[0:32, :] = came[104:136, :] + far[...]
    pick(x, slots, line, 32)
    line[64:96, :] = fore[...] + lent_next[...]


def list_kernel(count_ref, pairs_ref, out_ref, out, sem):
    lane = lax.broadcasted_iota(i32, (1, 256), 1)
    code = jnp.where(lane < count_ref[0, 0], pairs_ref[1:2, :] * NB + pairs_ref[0:1, :], 255)
    rows = 224
    c = lax.broadcasted_iota(i32, (rows, 256), 0)
    hit = jnp.where(code == c, 1.0, 0.0).astype(bf16)
    often = jnp.dot(hit, jnp.ones((256, 128), bf16), preferred_element_type=f32)
    ci = lax.broadcasted_iota(i32, (rows, 128), 0)
    there = (often > 0.5) & (ci < NT)
    r = lax.broadcasted_iota(i32, (rows, rows), 0)
    q = lax.broadcasted_iota(i32, (rows, rows), 1)
    rank = jnp.dot(
        jnp.where(q < r, 1.0, 0.0).astype(bf16),
        jnp.where(there, 1.0, 0.0).astype(bf16),
        preferred_element_type=f32,
    )
    cf = ci.astype(f32)
    for half in range(2):
        e = lax.broadcasted_iota(i32, (rows, 128), 1).astype(f32) + 128.0 * half
        pick = there & (rank == e)
        sl = slice(128 * half, 128 * half + 128)
        out[0:1, sl] = jnp.sum(jnp.where(pick, cf, 0.0), 0, keepdims=True).astype(i32)
        out[1:2, sl] = jnp.sum(jnp.where(pick, often, 0.0), 0, keepdims=True).astype(i32)
        out[2:3, sl] = rank[64:65].astype(i32)
        out[3:4, sl] = rank[NT : NT + 1].astype(i32)
    copy = pltpu.make_async_copy(out, out_ref, sem)
    copy.start()
    copy.wait()


def split3(f):
    h = f.astype(bf16)
    r = f - h.astype(f32)
    m = r.astype(bf16)
    return h, m, (r - m.astype(f32)).astype(bf16)


def cross(a, b):
    return [
        a[1] * b[2] - a[2] * b[1],
        a[2] * b[0] - a[0] * b[2],
        a[0] * b[1] - a[1] * b[0],
    ]


def dot3(a, b):
    return a[0] * b[0] + a[1] * b[1] + a[2] * b[2]


def scaled(get):
    x = [get(c) * SC for c in range(3)]
    v = [get(3 + c) for c in range(3)]
    r = get(12)
    u = [r * get(6 + c) for c in range(3)]
    return x, v, u, r * SC


def left_prep(get, ab, la, feat):
    x, v, u, rp = scaled(get)
    zero = jnp.zeros_like(rp)
    rows = x + v + u + [dot3(x, v), dot3(x, u), jnp.ones_like(rp), rp, zero, zero, zero]
    for n, q in enumerate(rows):
        feat[pl.ds(n, NB, stride=16), :] = q
    a = lax.broadcasted_iota(i32, (128, 128), 0)
    b = lax.broadcasted_iota(i32, (128, 128), 1)
    for i in range(NB):
        f = feat[16 * i : 16 * i + 16, :]
        h, m, l = (p.astype(f32) for p in split3(f))
        t = jnp.concatenate([h, h, m, m, h, l, f, jnp.zeros((16, 128), f32)], 0).T
        la[i] = jnp.where(b < 96, t, 0.0).astype(bf16)
        for n, c in enumerate((96, 97, 98, 108)):
            ab[i, n] = jnp.broadcast_to(t[:, c : c + 1], (128, 128))
        ab[i, 4] = jnp.where(a == b, 1e15, jnp.broadcast_to(t[:, 96:97], (128, 128)))


def right_prep(get, nb, at, rb, kb, wb, feat):
    x, v, u, rp = scaled(get)
    one = jnp.ones_like(rp)
    zero = jnp.zeros_like(rp)
    neg = lambda a: [-q for q in a]
    sb = jnp.sqrt(rp)
    s = neg(v) + neg(x) + [zero] * 3 + [one, zero, dot3(x, v)]
    t = u + [zero] * 3 + neg(x) + [zero, one, -dot3(x, u)]
    w = [sb * q for q in [one] + x + v + u + cross(u, x) + cross(x, v)]
    for k, rows in enumerate((s, t, w, x + [rp])):
        for n in range(16 if k < 3 else 4):
            feat[pl.ds(128 * k + n, nb, stride=16), :] = rows[n] if n < len(rows) else zero
    for p in range(nb):
        j = at[p]
        fs, ft, fw = (feat[128 * k + 16 * p : 128 * k + 16 * p + 16, :] for k in range(3))
        rb[j] = feat[384 + 16 * p : 384 + 16 * p + 8, :]
        sh, sm, sl = split3(fs)
        th, tm, tl = split3(ft)
        for n, (p0, p1) in enumerate(
            ((sh, th), (sm, tm), (sh, th), (sm, tm), (sl, tl), (sh, th))
        ):
            kb[j, 16 * n : 16 * n + 16, 0:128] = p0
            kb[j, 16 * n : 16 * n + 16, 128:256] = p1
        kb[j, 96:128, :] = jnp.zeros((32, 256), bf16)
        for n, p0 in enumerate(split3(fw)):
            wb[j, 16 * n : 16 * n + 16, 0:128] = p0
            wb[j, 16 * n : 16 * n + 16, 128:256] = p0


def tile_dots(i, j, la, kb, st):
    st[...] = jnp.dot(la[i], kb[j], preferred_element_type=f32)


def tile_terms(i, j, same, ab, st, rb, cf):
    xi = jnp.where(same, 4, 0)
    rows = 16
    right = [jnp.broadcast_to(rb[j, q : q + 1, :], (rows, 128)) for q in range(4)]
    for c in range(128 // rows):
        sl = slice(rows * c, rows * c + rows)
        dx = ab[i, xi, sl, :] - right[0]
        dy = ab[i, 1, sl, :] - right[1]
        dz = ab[i, 2, sl, :] - right[2]
        rs = ab[i, 3, sl, :] + right[3]
        d2 = jnp.minimum(dx * dx + dy * dy + dz * dz, 1e37)
        inv = lax.rsqrt(d2)
        depth = jnp.maximum(rs - d2 * inv, 0.0)
        rc = depth * lax.rsqrt(jnp.maximum(depth * rs, 1e-35))
        ga = rc * inv
        gi = ga * inv
        al = ga * depth - gi * st[sl, 0:128]
        de = gi * st[sl, 128:256]
        for n, co in enumerate((al, rc, ga, de)):
            h = co.astype(bf16)
            at = 128 * n + rows * c
            cf[at : at + rows, :] = h
            cf[512 + at : 512 + at + rows, :] = (co - h.astype(f32)).astype(bf16)


def tile_sums(i, j, mult, wb, cf, acc):
    both = jnp.concatenate([cf[0:512, :], cf[512:1024, :]], 1)
    o = lax.dot_general(wb[j], both, (((1,), (1,)), ((), ())), preferred_element_type=f32)
    o = (o[0:16] + o[16:32] + o[32:48]) * mult
    for q in range(4):
        at = pl.ds(pl.multiple_of(i * 16, 16) + 128 * q, 16)
        acc[at, :] = acc[at, :] + o[:, 128 * q : 128 * q + 128]


def tile_loop(start, stop, list_ref, ab, la, rb, kb, wb, cfs, sts, acc, base_j=0):
    def get(e):
        live = e < stop
        code = jnp.where(live, list_ref[0, e], 8 * base_j)
        often = jnp.where(live, list_ref[1, e], 0)
        return code & 7, (code >> 3) - base_j, often.astype(f32)

    trips = (stop - start + U - 1) // U
    for n in range(U - LAG, U):
        cfs[n][...] = jnp.zeros_like(cfs[n])
    for n in range(U):
        i, j, _ = get(start + n)
        tile_dots(i, j, la, kb, sts[n])

    def body(t, late):
        base = start + U * t
        late = list(late)
        for n in range(U):
            i, j, mult = get(base + n)
            tile_terms(i, j, i == j + base_j, ab, sts[n], rb, cfs[n])
            late.append((i, j, mult))
            i, j, mult = late.pop(0)
            tile_sums(i, j, mult, wb, cfs[(n - LAG) % U], acc)
            i, j, _ = get(base + U + n)
            tile_dots(i, j, la, kb, sts[n])
        return tuple(late)

    none = (jnp.int32(0), jnp.int32(0), jnp.float32(0))
    late = lax.fori_loop(0, trips, body, (none,) * LAG)
    for n, (i, j, mult) in enumerate(late):
        tile_sums(i, j, mult, wb, cfs[U - LAG + n], acc)


def own_kernel(list_ref, d, ab, la, acc, rb, kb, wb, feat, *bufs):
    left_prep(lambda c: d[c], ab, la, feat)
    right_prep(lambda c: d[c], NB, range(NB), rb, kb, wb, feat)
    acc[...] = jnp.zeros_like(acc)
    tile_loop(jnp.int32(0), list_ref[2, 0], list_ref, ab, la, rb, kb, wb, bufs[:U], bufs[U:], acc)


def ghost_kernel(list_ref, d, ab, la, part, below, line, above, out, acc, rb, kb, wb, feat, *bufs):
    acc[...] = part[...]
    for ref, lo in ((below, 0), (line, 6), (above, 12)):
        right_prep(lambda c: ref[pl.ds(c, 6, stride=16), :], 6, range(lo, lo + 6), rb, kb, wb, feat)
    tile_loop(
        list_ref[2, 0], list_ref[3, 0], list_ref, ab, la, rb, kb, wb, bufs[:U], bufs[U:], acc, NB
    )
    finish(d, acc, out)


def finish(d, acc, out):
    need = (4, 10, 16, 4)
    a, b, g, e = (
        [acc[pl.ds(128 * q + r, NB, stride=16), :] for r in range(need[q])]
        for q in range(4)
    )
    x, v, u, rp = scaled(lambda c: d[c])
    uxg = cross(u, g[1:4])
    ux = cross(u, x)
    gux = cross(g[7:10], x)
    xv = cross(x, v)
    xgv = cross(x, g[4:7])
    gxv = cross(g[1:4], v)
    r = d[12]
    mass = (DENSITY * (4.0 / 3.0) * jnp.pi) * (r * r * r)
    inertia = 0.4 * mass * r * r
    half = 0.5 * jnp.sqrt(rp)
    to_acc = half / mass
    to_ang = half * r * DT / inertia
    for c in range(3):
        force = (
            x[c] * (a[0] - g[0])
            - (a[1 + c] - g[1 + c])
            - (v[c] * b[0] - b[4 + c])
            + (ux[c] * g[0] - uxg[c] + gux[c] - g[10 + c])
        )
        torque = (
            (xv[c] * g[0] - xgv[c] - gxv[c] + g[13 + c])
            - (u[c] * b[0] + b[7 + c])
            + (x[c] * e[0] - e[1 + c])
        )
        accel = force * to_acc
        if c == 2:
            accel = accel - 1.0
        out[c] = d[c]
        out[3 + c] = v[c] + (0.5 * DT) * (d[9 + c] + accel)
        out[6 + c] = d[6 + c] + torque * to_ang
        out[9 + c] = accel
    out[12] = r


VM = pl.BlockSpec(memory_space=pltpu.VMEM)
SM = pl.BlockSpec(memory_space=pltpu.SMEM)


def kernel_call(body, ins, outs, scratch=()):
    kinds = {"smem": pltpu.SMEM, "vmem": pltpu.VMEM, "sfar": pltpu.HBM, "hbm": pltpu.HBM}
    args = [
        pltpu.with_memory_space_constraint(x, kinds[space]) if space in kinds else x
        for x, space in ins
    ]
    return pl.pallas_call(
        body,
        out_shape=outs,
        in_specs=[SM if space in ("smem", "sfar", "scalar") else VM for _, space in ins],
        out_specs=tuple(
            SM if getattr(o, "memory_space", None) == pltpu.SMEM else VM for o in outs
        ),
        scratch_shapes=list(scratch),
        compiler_params=pltpu.CompilerParams(vmem_limit_bytes=16 << 20),
    )(*args)


WORK = [pltpu.VMEM((1024, 128), bf16)] * U + [pltpu.VMEM((128, 256), f32)] * U
FEAT = pltpu.VMEM((512, 128), f32)
SUMS = pltpu.VMEM((4 * NB * 16, 128), f32)


def right_refs(n):
    return [
        pltpu.VMEM((n, 8, 128), f32),
        pltpu.VMEM((n, 128, 256), bf16),
        pltpu.VMEM((n, 48, 256), bf16),
        FEAT,
    ]


def own_call(order, drifted):
    return kernel_call(
        own_kernel,
        [(order, "smem"), (drifted, "vmem")],
        (pltpu.VMEM((NB, 5, 128, 128), f32), pltpu.VMEM((NB, 128, 128), bf16), SUMS),
        right_refs(NB) + WORK,
    )


def ghost_call(order, drifted, made, below, line, above):
    ab, la, part = made
    (out,) = kernel_call(
        ghost_kernel,
        [(order, "smem")] + [(x, "vmem") for x in (drifted, ab, la, part, below, line, above)],
        (jax.ShapeDtypeStruct((13, NB, 128), f32),),
        [SUMS] + right_refs(18) + WORK,
    )
    return out


def one_step(spheres, new_home, ghost_list, tile_pairs, tile_count):
    block = pltpu.VMEM((13, NB, 128), f32)
    pair = pltpu.VMEM((32, 128), f32)
    mine, slots = kernel_call(
        embed_kernel,
        [(new_home, "sfar"), (ghost_list, "sfar"), (spheres.reshape(13, NB, 128), "hbm")],
        (pltpu.VMEM((14, NB, 128), f32), pltpu.VMEM((NB, 128), f32)),
    )
    past = passed_along(mine, "gx", 2)
    next_slots = passed_along(slots, "gx", -1)
    (order,) = kernel_call(
        list_kernel,
        [(tile_count, "scalar"), (tile_pairs[0].T, "hbm")],
        (pltpu.SMEM((8, 256), i32),),
        [pltpu.VMEM((8, 256), i32), pltpu.SemaphoreType.DMA(())],
    )
    order, past, next_slots = lax.optimization_barrier((order, past, next_slots))
    keep, ship, lent, lent_next = kernel_call(
        sort_kernel,
        [(x, "vmem") for x in (mine, past, slots, next_slots)],
        (block, pltpu.VMEM((136, 128), f32), pair, pair),
    )
    far = passed_along(lent_next, "gx", 2)
    came = passed_along(ship, "gx", 1)
    fore = passed_along(lent, "gx", -1)
    drifted, line = kernel_call(
        join_kernel,
        [(x, "vmem") for x in (keep, came, far, fore, lent_next, slots)],
        (block, pltpu.VMEM((96, 128), f32)),
    )
    below = passed_along(line, "gy", 1)
    above = passed_along(line, "gy", -1)
    made = own_call(order, drifted)
    return ghost_call(order, drifted, made, below, line, above)[:, None]


def solution(mesh):
    in_specs = (
        P(None, "gy", "gx", None),
        P("gy", "gx"),
        P("gy", "gx"),
        P("gy", "gx", None),
        P("gy", "gx"),
    )
    return jax.shard_map(
        one_step,
        mesh=mesh,
        in_specs=in_specs,
        out_specs=P(None, "gy", "gx", None),
        check_vma=False,
    )
```

profile of v0, /device:TPU:1, one launch (start us, length us, event | category | flops | bytes accessed | tf_op | source)
XLA Modules:
  0.0 41.1 jit_solution(2960967080241606099)
XLA Ops:
  0.0 0.8 %shard_map.56 = (f32[14,8,128]{2,1,0:T(8,128)S(1)}, f32[8,128]{1,0:T(8,128)S(1)}) custom-call(s32[1,8]{1,0:T(1,128)} %home_ref.1, s32[1,2]{1,0:T(1,128)} %lent_ref.1, f32[13,8,128]{2,1,0:T(8,128)} %bitcast.7), custom_call_target="tpu_custom_call" | custom-call | tf_op jit(solution)/shard_map/pallas_call | solution.py:332
  0.8 3.9 %collective-permute-start = (f32[14,8,128]{2,1,0:T(8,128)S(1)}, f32[14,8,128]{2,1,0:T(8,128)S(1)}, u32[]{:S(2)}, u32[]{:S(2)}) collective-permute-start(f32[14,8,128]{2,1,0:T(8,128)S(1)} %get-tuple-element.19.mine), channel_id=1, source_target_pairs={{0,16},{8,24},{16,32},{24,40},{32,48},{40,56},{48,64},{56,72},{64,... | collective-permute-start | bytes 172040 | tf_op jit(solution)/shard_map/ppermute | solution.py:25
  4.7 4.9 %collective-permute-start.1 = (f32[8,128]{1,0:T(8,128)S(1)}, f32[8,128]{1,0:T(8,128)S(1)}, u32[]{:S(2)}, u32[]{:S(2)}) collective-permute-start(f32[8,128]{1,0:T(8,128)S(1)} %get-tuple-element.20.slots), channel_id=1, source_target_pairs={{0,248},{8,0},{16,8},{24,16},{32,24},{40,32},{48,40},{56,48},{64,5... | collective-permute-start | bytes 12296 | tf_op jit(solution)/shard_map/ppermute | solution.py:25
  10.2 1.7 %shard_map.55.list_ref = s32[8,256]{1,0:T(8,128)S(4)} custom-call(s32[1,1]{1,0:T(1,128)S(6)} %copy.7.count_ref, s32[2,256]{1,0:T(2,128)} %bitcast.8), custom_call_target="tpu_custom_call" | custom-call | tf_op jit(solution)/shard_map/pallas_call | solution.py:332
  12.0 0.0 collective-permute-done.1.next_slots
  12.0 0.0 collective-permute-done.past
  12.0 0.2 shard_map.57
  12.2 1.3 %collective-permute-start.2 = (f32[136,128]{1,0:T(8,128)S(1)}, f32[136,128]{1,0:T(8,128)S(1)}, u32[]{:S(2)}, u32[]{:S(2)}) collective-permute-start(f32[136,128]{1,0:T(8,128)S(1)} %get-tuple-element.25), channel_id=1, source_target_pairs={{0,8},{8,16},{16,24},{24,32},{32,40},{40,48},{48,56},{56,64},{64,7... | collective-permute-start | bytes 208904 | tf_op jit(solution)/shard_map/ppermute | solution.py:25
  13.5 3.6 %collective-permute-start.4 = (f32[32,128]{1,0:T(8,128)S(1)}, f32[32,128]{1,0:T(8,128)S(1)}, u32[]{:S(2)}, u32[]{:S(2)}) collective-permute-start(f32[32,128]{1,0:T(8,128)S(1)} %get-tuple-element.27), channel_id=1, source_target_pairs={{0,248},{8,0},{16,8},{24,16},{32,24},{40,32},{48,40},{56,48},{64,5... | collective-permute-start | bytes 49160 | tf_op jit(solution)/shard_map/ppermute | solution.py:25
  17.1 0.0 collective-permute-start.3
  17.1 0.9 %collective-permute-done.4.fore = f32[32,128]{1,0:T(8,128)S(1)} collective-permute-done((f32[32,128]{1,0:T(8,128)S(1)}, f32[32,128]{1,0:T(8,128)S(1)}, u32[]{:S(2)}, u32[]{:S(2)}) %collective-permute-start.4) | collective-permute-done | bytes 16416 | tf_op jit(solution)/shard_map/ppermute | solution.py:25
  17.9 5.9 %collective-permute-done.3.far = f32[32,128]{1,0:T(8,128)S(1)} collective-permute-done((f32[32,128]{1,0:T(8,128)S(1)}, f32[32,128]{1,0:T(8,128)S(1)}, u32[]{:S(2)}, u32[]{:S(2)}) %collective-permute-start.3) | collective-permute-done | bytes 16416 | tf_op jit(solution)/shard_map/ppermute | solution.py:25
  23.9 0.0 collective-permute-done.2.came
  23.9 2.8 %collective-permute-start.6 = (f32[96,128]{1,0:T(8,128)S(1)}, f32[96,128]{1,0:T(8,128)S(1)}, u32[]{:S(2)}, u32[]{:S(2)}) collective-permute-start(f32[96,128]{1,0:T(8,128)S(1)} %get-tuple-element.32.line), channel_id=1, source_target_pairs={{0,7},{1,0},{2,1},{3,2},{4,3},{5,4},{6,5},{7,6},{8,15},{9,8},{10,9... | collective-permute-start | bytes 147464 | tf_op jit(solution)/shard_map/ppermute | solution.py:25
  26.7 1.2 %collective-permute-start.5 = (f32[96,128]{1,0:T(8,128)S(1)}, f32[96,128]{1,0:T(8,128)S(1)}, u32[]{:S(2)}, u32[]{:S(2)}) collective-permute-start(f32[96,128]{1,0:T(8,128)S(1)} %get-tuple-element.32.line), channel_id=1, source_target_pairs={{0,1},{1,2},{2,3},{3,4},{4,5},{5,6},{6,7},{7,0},{8,9},{9,10},{10,1... | collective-permute-start | bytes 147464 | tf_op jit(solution)/shard_map/ppermute | solution.py:25
  27.9 5.0 %shard_map.59 = (f32[8,5,128,128]{3,2,1,0:T(8,128)S(1)}, bf16[8,128,128]{2,1,0:T(8,128)(2,1)S(1)}, f32[512,128]{1,0:T(8,128)S(1)}) custom-call(s32[8,256]{1,0:T(8,128)S(4)} %shard_map.55.list_ref, f32[13,8,128]{2,1,0:T(8,128)S(1)} %get-tuple-element.28.d), custom_call_target="tpu_custom_call" | custom-call | tf_op jit(solution)/shard_map/pallas_call | solution.py:332
  32.9 0.0 collective-permute-done.6.above
  32.9 0.0 collective-permute-done.5.below
  32.9 8.1 %shard_map.60 = f32[13,8,128]{2,1,0:T(8,128)} custom-call(s32[8,256]{1,0:T(8,128)S(4)} %shard_map.55.list_ref, f32[13,8,128]{2,1,0:T(8,128)S(1)} %get-tuple-element.28.d, f32[8,5,128,128]{3,2,1,0:T(8,128)S(1)} %get-tuple-element.29.ab, bf16[8,128,128]{2,1,0:T(8,128)(2,1)S(1)} %get-tuple-element.30.la, f32[512,128]{1,0:T(8,128)S(1)} %get-tuple-element.31.part, ...), custom_call_target="tpu_custom_call" | custom-call | tf_op jit(solution)/shard_map/pallas_call | solution.py:332
  (1 shorter events, 0.0 us)
Async XLA Ops:
  0.8 11.2 %collective-permute-start = (f32[14,8,128]{2,1,0:T(8,128)S(1)}, f32[14,8,128]{2,1,0:T(8,128)S(1)}, u32[]{:S(2)}, u32[]{:S(2)}) collective-permute-start(f32[14,8,128]{2,1,0:T(8,128)S(1)} %get-tuple-element.19.mine), channel_id=1, source_target_pairs={{0,16},{8,24},{16,32},{24,40},{32,48},{40,56},{48,64},{56,72},{64,... | collective-permute-start | bytes 172040 | tf_op jit(solution)/shard_map/ppermute | solution.py:25
  4.7 7.3 %collective-permute-start.1 = (f32[8,128]{1,0:T(8,128)S(1)}, f32[8,128]{1,0:T(8,128)S(1)}, u32[]{:S(2)}, u32[]{:S(2)}) collective-permute-start(f32[8,128]{1,0:T(8,128)S(1)} %get-tuple-element.20.slots), channel_id=1, source_target_pairs={{0,248},{8,0},{16,8},{24,16},{32,24},{40,32},{48,40},{56,48},{64,5... | collective-permute-start | bytes 12296 | tf_op jit(solution)/shard_map/ppermute | solution.py:25
  12.2 11.7 %collective-permute-start.2 = (f32[136,128]{1,0:T(8,128)S(1)}, f32[136,128]{1,0:T(8,128)S(1)}, u32[]{:S(2)}, u32[]{:S(2)}) collective-permute-start(f32[136,128]{1,0:T(8,128)S(1)} %get-tuple-element.25), channel_id=1, source_target_pairs={{0,8},{8,16},{16,24},{24,32},{32,40},{40,48},{48,56},{56,64},{64,7... | collective-permute-start | bytes 208904 | tf_op jit(solution)/shard_map/ppermute | solution.py:25
  13.5 4.4 %collective-permute-start.4 = (f32[32,128]{1,0:T(8,128)S(1)}, f32[32,128]{1,0:T(8,128)S(1)}, u32[]{:S(2)}, u32[]{:S(2)}) collective-permute-start(f32[32,128]{1,0:T(8,128)S(1)} %get-tuple-element.27), channel_id=1, source_target_pairs={{0,248},{8,0},{16,8},{24,16},{32,24},{40,32},{48,40},{56,48},{64,5... | collective-permute-start | bytes 49160 | tf_op jit(solution)/shard_map/ppermute | solution.py:25
  17.1 6.8 %collective-permute-start.3 = (f32[32,128]{1,0:T(8,128)S(1)}, f32[32,128]{1,0:T(8,128)S(1)}, u32[]{:S(2)}, u32[]{:S(2)}) collective-permute-start(f32[32,128]{1,0:T(8,128)S(1)} %get-tuple-element.26.lent_next), channel_id=1, source_target_pairs={{0,16},{8,24},{16,32},{24,40},{32,48},{40,56},{48,64},{56,72},{64,... | collective-permute-start | bytes 49160 | tf_op jit(solution)/shard_map/ppermute | solution.py:25
  23.9 9.0 %collective-permute-start.6 = (f32[96,128]{1,0:T(8,128)S(1)}, f32[96,128]{1,0:T(8,128)S(1)}, u32[]{:S(2)}, u32[]{:S(2)}) collective-permute-start(f32[96,128]{1,0:T(8,128)S(1)} %get-tuple-element.32.line), channel_id=1, source_target_pairs={{0,7},{1,0},{2,1},{3,2},{4,3},{5,4},{6,5},{7,6},{8,15},{9,8},{10,9... | collective-permute-start | bytes 147464 | tf_op jit(solution)/shard_map/ppermute | solution.py:25
  26.7 6.2 %collective-permute-start.5 = (f32[96,128]{1,0:T(8,128)S(1)}, f32[96,128]{1,0:T(8,128)S(1)}, u32[]{:S(2)}, u32[]{:S(2)}) collective-permute-start(f32[96,128]{1,0:T(8,128)S(1)} %get-tuple-element.32.line), channel_id=1, source_target_pairs={{0,1},{1,2},{2,3},{3,4},{4,5},{5,6},{6,7},{7,0},{8,9},{9,10},{10,1... | collective-permute-start | bytes 147464 | tf_op jit(solution)/shard_map/ppermute | solution.py:25
where the time goes:
time: 41.2 us; the launch traced here: 41.1 us
  starting transfers between devices  17.6 us (43%)
  Pallas kernels  15.9 us (39%)
  waiting for transfers between devices  6.85 us (17%)
  between operations  0.7 us (2%)
    ppermute x7, starting transfers between devices, passed_along(): return lax.ppermute(x, axis, [(i, (i + by) % peers) for i in range(peers)])  17.6 us
    pallas_call x6, Pallas kernels, kernel_call(): pl.pallas_call(body, out_shape=outs, in_specs=[SM if space in ('smem', 's...  15.9 us
    ppermute x7, waiting for transfers between devices, passed_along(): return lax.ppermute(x, axis, [(i, (i + by) % peers) for i in range(peers)])  6.85 us
  transfers between devices with their start and end apart: 7, of which 2 were waited for; matrix products, arithmetic and copies ran while one was open for 0% of the time, Pallas kernels for 16%

commit v1 on v0

--- a/solution.py
+++ b/solution.py
@@ -12,8 +12,9 @@
 NB = 8
 NP = 26
 NT = NB * NP
-U = 8
-LAG = 2
+U = 12
+AHEAD = 2
+LAG = 1
 
 f32 = jnp.float32
 bf16 = jnp.bfloat16
@@ -93,8 +94,17 @@
     c = lax.broadcasted_iota(i32, (rows, 256), 0)
     hit = jnp.where(code == c, 1.0, 0.0).astype(bf16)
     often = jnp.dot(hit, jnp.ones((256, 128), bf16), preferred_element_type=f32)
+    co = lax.broadcasted_iota(i32, (64, 256), 0)
+    mirror = jnp.dot(
+        jnp.where(code == ((co & 7) << 3) + (co >> 3), 1.0, 0.0).astype(bf16),
+        jnp.ones((256, 128), bf16),
+        preferred_element_type=f32,
+    )
+    mirror = jnp.concatenate([mirror, jnp.zeros((rows - 64, 128), f32)], 0)
     ci = lax.broadcasted_iota(i32, (rows, 128), 0)
-    there = (often > 0.5) & (ci < NT)
+    first, second = ci & 7, ci >> 3
+    mirror = jnp.where(first < second, mirror, 0.0)
+    there = (often + mirror > 0.5) & (ci < NT) & (first <= second)
     r = lax.broadcasted_iota(i32, (rows, rows), 0)
     q = lax.broadcasted_iota(i32, (rows, rows), 1)
     rank = jnp.dot(
@@ -109,8 +119,9 @@
         sl = slice(128 * half, 128 * half + 128)
         out[0:1, sl] = jnp.sum(jnp.where(pick, cf, 0.0), 0, keepdims=True).astype(i32)
         out[1:2, sl] = jnp.sum(jnp.where(pick, often, 0.0), 0, keepdims=True).astype(i32)
-        out[2:3, sl] = rank[64:65].astype(i32)
-        out[3:4, sl] = rank[NT : NT + 1].astype(i32)
+        out[2:3, sl] = jnp.sum(jnp.where(pick, mirror, 0.0), 0, keepdims=True).astype(i32)
+        out[3:4, sl] = rank[64:65].astype(i32)
+        out[4:5, sl] = rank[NT : NT + 1].astype(i32)
     copy = pltpu.make_async_copy(out, out_ref, sem)
     copy.start()
     copy.wait()
@@ -219,53 +230,76 @@
             cf[512 + at : 512 + at + rows, :] = (co - h.astype(f32)).astype(bf16)
 
 
+def add_sums(o, i, mult, acc, flip):
+    o = o[0:16] + o[16:32] + o[32:48]
+    for q in range(4):
+        at = pl.ds(pl.multiple_of(i * 16, 16) + 128 * q, 16)
+        part = o[:, 128 * q : 128 * q + 128] * mult
+        acc[at, :] = acc[at, :] - part if flip and q == 3 else acc[at, :] + part
+
+
 def tile_sums(i, j, mult, wb, cf, acc):
     both = jnp.concatenate([cf[0:512, :], cf[512:1024, :]], 1)
     o = lax.dot_general(wb[j], both, (((1,), (1,)), ((), ())), preferred_element_type=f32)
-    o = (o[0:16] + o[16:32] + o[32:48]) * mult
-    for q in range(4):
-        at = pl.ds(pl.multiple_of(i * 16, 16) + 128 * q, 16)
-        acc[at, :] = acc[at, :] + o[:, 128 * q : 128 * q + 128]
-
-
-def tile_loop(start, stop, list_ref, ab, la, rb, kb, wb, cfs, sts, acc, base_j=0):
+    add_sums(o, i, mult, acc, False)
+
+
+def mirror_sums(i, j, mult, wb, cf, acc):
+    cols = [
+        jnp.concatenate([cf[128 * q : 128 * q + 128, :], cf[512 + 128 * q : 640 + 128 * q, :]], 0)
+        for q in range(4)
+    ]
+    o = jnp.dot(wb[i], jnp.concatenate(cols, 1), preferred_element_type=f32)
+    add_sums(o, j, mult, acc, True)
+
+
+def tile_loop(start, stop, list_ref, ab, la, rb, kb, wb, cfs, sts, acc, base_j=0, both=False):
     def get(e):
         live = e < stop
         code = jnp.where(live, list_ref[0, e], 8 * base_j)
         often = jnp.where(live, list_ref[1, e], 0)
-        return code & 7, (code >> 3) - base_j, often.astype(f32)
+        mirror = jnp.where(live, list_ref[2, e], 0) if both else 0
+        return code & 7, (code >> 3) - base_j, often.astype(f32), jnp.asarray(mirror, f32)
+
+    def sums(tile, cf):
+        i, j, mult, mirror = tile
+        tile_sums(i, j, mult, wb, cf, acc)
+        if both:
+            mirror_sums(i, j, mirror, wb, cf, acc)
 
     trips = (stop - start + U - 1) // U
     for n in range(U - LAG, U):
         cfs[n][...] = jnp.zeros_like(cfs[n])
-    for n in range(U):
-        i, j, _ = get(start + n)
+    for n in range(AHEAD):
+        i, j, _, _ = get(start + n)
         tile_dots(i, j, la, kb, sts[n])
 
     def body(t, late):
         base = start + U * t
         late = list(late)
         for n in range(U):
-            i, j, mult = get(base + n)
+            tile = get(base + n)
+            i, j = tile[:2]
             tile_terms(i, j, i == j + base_j, ab, sts[n], rb, cfs[n])
-            late.append((i, j, mult))
-            i, j, mult = late.pop(0)
-            tile_sums(i, j, mult, wb, cfs[(n - LAG) % U], acc)
-            i, j, _ = get(base + U + n)
-            tile_dots(i, j, la, kb, sts[n])
+            late.append(tile)
+            sums(late.pop(0), cfs[(n - LAG) % U])
+            i, j, _, _ = get(base + n + AHEAD)
+            tile_dots(i, j, la, kb, sts[(n + AHEAD) % U])
         return tuple(late)
 
-    none = (jnp.int32(0), jnp.int32(0), jnp.float32(0))
+    none = (jnp.int32(0), jnp.int32(0), jnp.float32(0), jnp.float32(0))
     late = lax.fori_loop(0, trips, body, (none,) * LAG)
-    for n, (i, j, mult) in enumerate(late):
-        tile_sums(i, j, mult, wb, cfs[U - LAG + n], acc)
+    for n, tile in enumerate(late):
+        sums(tile, cfs[U - LAG + n])
 
 
 def own_kernel(list_ref, d, ab, la, acc, rb, kb, wb, feat, *bufs):
     left_prep(lambda c: d[c], ab, la, feat)
     right_prep(lambda c: d[c], NB, range(NB), rb, kb, wb, feat)
     acc[...] = jnp.zeros_like(acc)
-    tile_loop(jnp.int32(0), list_ref[2, 0], list_ref, ab, la, rb, kb, wb, bufs[:U], bufs[U:], acc)
+    tile_loop(
+        jnp.int32(0), list_ref[3, 0], list_ref, ab, la, rb, kb, wb, bufs[:U], bufs[U:], acc, both=True
+    )
 
 
 def ghost_kernel(list_ref, d, ab, la, part, below, line, above, out, acc, rb, kb, wb, feat, *bufs):
@@ -273,7 +307,7 @@
     for ref, lo in ((below, 0), (line, 6), (above, 12)):
         right_prep(lambda c: ref[pl.ds(c, 6, stride=16), :], 6, range(lo, lo + 6), rb, kb, wb, feat)
     tile_loop(
-        list_ref[2, 0], list_ref[3, 0], list_ref, ab, la, rb, kb, wb, bufs[:U], bufs[U:], acc, NB
+        list_ref[3, 0], list_ref[4, 0], list_ref, ab, la, rb, kb, wb, bufs[:U], bufs[U:], acc, NB
     )
     finish(d, acc, out)
 

time: 41.2 us -> 42.5 us (1.032)
  Pallas kernels: 15.9 us -> 17.3 us
    pallas_call x6, Pallas kernels: 15.9 us -> 17.3 us  [kernel_call(): pl.pallas_call(body, out_shape=outs, in_specs=[SM if space in ('smem', 's...]
  transfers between devices with their start and end apart: 7 -> 7, of which waited for: 2 -> 2; matrix products, arithmetic and copies ran while one was open for 0% -> 0% of each run, Pallas kernels for 16% -> 19%
where the time goes in v1:
time: 42.5 us; the launch traced here: 42.4 us
  starting transfers between devices  17.6 us (41%)
  Pallas kernels  17.3 us (41%)
  waiting for transfers between devices  6.83 us (16%)
  between operations  0.71 us (2%)
    ppermute x7, starting transfers between devices, passed_along(): return lax.ppermute(x, axis, [(i, (i + by) % peers) for i in range(peers)])  17.6 us
    pallas_call x6, Pallas kernels, kernel_call(): pl.pallas_call(body, out_shape=outs, in_specs=[SM if space in ('smem', 's...  17.3 us
    ppermute x7, waiting for transfers between devices, passed_along(): return lax.ppermute(x, axis, [(i, (i + by) % peers) for i in range(peers)])  6.83 us
  transfers between devices with their start and end apart: 7, of which 2 were waited for; matrix products, arithmetic and copies ran while one was open for 0% of the time, Pallas kernels for 19%

profile of v1, /device:TPU:1, one launch (start us, length us, event | category | flops | bytes accessed | tf_op | source)
XLA Modules:
  0.0 42.4 jit_solution(5293220805618417731)
XLA Ops:
  0.0 0.8 %shard_map.56 = (f32[14,8,128]{2,1,0:T(8,128)S(1)}, f32[8,128]{1,0:T(8,128)S(1)}) custom-call(s32[1,8]{1,0:T(1,128)} %home_ref.1, s32[1,2]{1,0:T(1,128)} %lent_ref.1, f32[13,8,128]{2,1,0:T(8,128)} %bitcast.7), custom_call_target="tpu_custom_call" | custom-call | tf_op jit(solution)/shard_map/pallas_call | solution.py:366
  0.8 3.9 %collective-permute-start = (f32[14,8,128]{2,1,0:T(8,128)S(1)}, f32[14,8,128]{2,1,0:T(8,128)S(1)}, u32[]{:S(2)}, u32[]{:S(2)}) collective-permute-start(f32[14,8,128]{2,1,0:T(8,128)S(1)} %get-tuple-element.19.mine), channel_id=1, source_target_pairs={{0,16},{8,24},{16,32},{24,40},{32,48},{40,56},{48,64},{56,72},{64,... | collective-permute-start | bytes 172040 | tf_op jit(solution)/shard_map/ppermute | solution.py:26
  4.7 4.9 %collective-permute-start.1 = (f32[8,128]{1,0:T(8,128)S(1)}, f32[8,128]{1,0:T(8,128)S(1)}, u32[]{:S(2)}, u32[]{:S(2)}) collective-permute-start(f32[8,128]{1,0:T(8,128)S(1)} %get-tuple-element.20.slots), channel_id=1, source_target_pairs={{0,248},{8,0},{16,8},{24,16},{32,24},{40,32},{48,40},{56,48},{64,5... | collective-permute-start | bytes 12296 | tf_op jit(solution)/shard_map/ppermute | solution.py:26
  10.2 1.7 %shard_map.55.list_ref = s32[8,256]{1,0:T(8,128)S(4)} custom-call(s32[1,1]{1,0:T(1,128)S(6)} %copy.7.count_ref, s32[2,256]{1,0:T(2,128)} %bitcast.8), custom_call_target="tpu_custom_call" | custom-call | tf_op jit(solution)/shard_map/pallas_call | solution.py:366
  12.0 0.0 collective-permute-done.1.next_slots
  12.0 0.0 collective-permute-done.past
  12.0 0.2 shard_map.57
  12.2 1.3 %collective-permute-start.2 = (f32[136,128]{1,0:T(8,128)S(1)}, f32[136,128]{1,0:T(8,128)S(1)}, u32[]{:S(2)}, u32[]{:S(2)}) collective-permute-start(f32[136,128]{1,0:T(8,128)S(1)} %get-tuple-element.25), channel_id=1, source_target_pairs={{0,8},{8,16},{16,24},{24,32},{32,40},{40,48},{48,56},{56,64},{64,7... | collective-permute-start | bytes 208904 | tf_op jit(solution)/shard_map/ppermute | solution.py:26
  13.5 3.6 %collective-permute-start.4 = (f32[32,128]{1,0:T(8,128)S(1)}, f32[32,128]{1,0:T(8,128)S(1)}, u32[]{:S(2)}, u32[]{:S(2)}) collective-permute-start(f32[32,128]{1,0:T(8,128)S(1)} %get-tuple-element.27), channel_id=1, source_target_pairs={{0,248},{8,0},{16,8},{24,16},{32,24},{40,32},{48,40},{56,48},{64,5... | collective-permute-start | bytes 49160 | tf_op jit(solution)/shard_map/ppermute | solution.py:26
  17.1 0.0 collective-permute-start.3
  17.1 0.9 %collective-permute-done.4.fore = f32[32,128]{1,0:T(8,128)S(1)} collective-permute-done((f32[32,128]{1,0:T(8,128)S(1)}, f32[32,128]{1,0:T(8,128)S(1)}, u32[]{:S(2)}, u32[]{:S(2)}) %collective-permute-start.4) | collective-permute-done | bytes 16416 | tf_op jit(solution)/shard_map/ppermute | solution.py:26
  17.9 5.9 %collective-permute-done.3.far = f32[32,128]{1,0:T(8,128)S(1)} collective-permute-done((f32[32,128]{1,0:T(8,128)S(1)}, f32[32,128]{1,0:T(8,128)S(1)}, u32[]{:S(2)}, u32[]{:S(2)}) %collective-permute-start.3) | collective-permute-done | bytes 16416 | tf_op jit(solution)/shard_map/ppermute | solution.py:26
  23.9 0.0 collective-permute-done.2.came
  23.9 2.8 %collective-permute-start.6 = (f32[96,128]{1,0:T(8,128)S(1)}, f32[96,128]{1,0:T(8,128)S(1)}, u32[]{:S(2)}, u32[]{:S(2)}) collective-permute-start(f32[96,128]{1,0:T(8,128)S(1)} %get-tuple-element.32.line), channel_id=1, source_target_pairs={{0,7},{1,0},{2,1},{3,2},{4,3},{5,4},{6,5},{7,6},{8,15},{9,8},{10,9... | collective-permute-start | bytes 147464 | tf_op jit(solution)/shard_map/ppermute | solution.py:26
  26.7 1.2 %collective-permute-start.5 = (f32[96,128]{1,0:T(8,128)S(1)}, f32[96,128]{1,0:T(8,128)S(1)}, u32[]{:S(2)}, u32[]{:S(2)}) collective-permute-start(f32[96,128]{1,0:T(8,128)S(1)} %get-tuple-element.32.line), channel_id=1, source_target_pairs={{0,1},{1,2},{2,3},{3,4},{4,5},{5,6},{6,7},{7,0},{8,9},{9,10},{10,1... | collective-permute-start | bytes 147464 | tf_op jit(solution)/shard_map/ppermute | solution.py:26
  27.9 6.3 %shard_map.59 = (f32[8,5,128,128]{3,2,1,0:T(8,128)S(1)}, bf16[8,128,128]{2,1,0:T(8,128)(2,1)S(1)}, f32[512,128]{1,0:T(8,128)S(1)}) custom-call(s32[8,256]{1,0:T(8,128)S(4)} %shard_map.55.list_ref, f32[13,8,128]{2,1,0:T(8,128)S(1)} %get-tuple-element.28.d), custom_call_target="tpu_custom_call" | custom-call | tf_op jit(solution)/shard_map/pallas_call | solution.py:366
  34.2 0.0 collective-permute-done.6.above
  34.2 0.0 collective-permute-done.5.below
  34.3 8.1 %shard_map.60 = f32[13,8,128]{2,1,0:T(8,128)} custom-call(s32[8,256]{1,0:T(8,128)S(4)} %shard_map.55.list_ref, f32[13,8,128]{2,1,0:T(8,128)S(1)} %get-tuple-element.28.d, f32[8,5,128,128]{3,2,1,0:T(8,128)S(1)} %get-tuple-element.29.ab, bf16[8,128,128]{2,1,0:T(8,128)(2,1)S(1)} %get-tuple-element.30.la, f32[512,128]{1,0:T(8,128)S(1)} %get-tuple-element.31.part, ...), custom_call_target="tpu_custom_call" | custom-call | tf_op jit(solution)/shard_map/pallas_call | solution.py:366
  (1 shorter events, 0.0 us)
Async XLA Ops:
  0.8 11.2 %collective-permute-start = (f32[14,8,128]{2,1,0:T(8,128)S(1)}, f32[14,8,128]{2,1,0:T(8,128)S(1)}, u32[]{:S(2)}, u32[]{:S(2)}) collective-permute-start(f32[14,8,128]{2,1,0:T(8,128)S(1)} %get-tuple-element.19.mine), channel_id=1, source_target_pairs={{0,16},{8,24},{16,32},{24,40},{32,48},{40,56},{48,64},{56,72},{64,... | collective-permute-start | bytes 172040 | tf_op jit(solution)/shard_map/ppermute | solution.py:26
  4.7 7.3 %collective-permute-start.1 = (f32[8,128]{1,0:T(8,128)S(1)}, f32[8,128]{1,0:T(8,128)S(1)}, u32[]{:S(2)}, u32[]{:S(2)}) collective-permute-start(f32[8,128]{1,0:T(8,128)S(1)} %get-tuple-element.20.slots), channel_id=1, source_target_pairs={{0,248},{8,0},{16,8},{24,16},{32,24},{40,32},{48,40},{56,48},{64,5... | collective-permute-start | bytes 12296 | tf_op jit(solution)/shard_map/ppermute | solution.py:26
  12.2 11.7 %collective-permute-start.2 = (f32[136,128]{1,0:T(8,128)S(1)}, f32[136,128]{1,0:T(8,128)S(1)}, u32[]{:S(2)}, u32[]{:S(2)}) collective-permute-start(f32[136,128]{1,0:T(8,128)S(1)} %get-tuple-element.25), channel_id=1, source_target_pairs={{0,8},{8,16},{16,24},{24,32},{32,40},{40,48},{48,56},{56,64},{64,7... | collective-permute-start | bytes 208904 | tf_op jit(solution)/shard_map/ppermute | solution.py:26
  13.5 4.4 %collective-permute-start.4 = (f32[32,128]{1,0:T(8,128)S(1)}, f32[32,128]{1,0:T(8,128)S(1)}, u32[]{:S(2)}, u32[]{:S(2)}) collective-permute-start(f32[32,128]{1,0:T(8,128)S(1)} %get-tuple-element.27), channel_id=1, source_target_pairs={{0,248},{8,0},{16,8},{24,16},{32,24},{40,32},{48,40},{56,48},{64,5... | collective-permute-start | bytes 49160 | tf_op jit(solution)/shard_map/ppermute | solution.py:26
  17.1 6.8 %collective-permute-start.3 = (f32[32,128]{1,0:T(8,128)S(1)}, f32[32,128]{1,0:T(8,128)S(1)}, u32[]{:S(2)}, u32[]{:S(2)}) collective-permute-start(f32[32,128]{1,0:T(8,128)S(1)} %get-tuple-element.26.lent_next), channel_id=1, source_target_pairs={{0,16},{8,24},{16,32},{24,40},{32,48},{40,56},{48,64},{56,72},{64,... | collective-permute-start | bytes 49160 | tf_op jit(solution)/shard_map/ppermute | solution.py:26
  23.9 10.3 %collective-permute-start.6 = (f32[96,128]{1,0:T(8,128)S(1)}, f32[96,128]{1,0:T(8,128)S(1)}, u32[]{:S(2)}, u32[]{:S(2)}) collective-permute-start(f32[96,128]{1,0:T(8,128)S(1)} %get-tuple-element.32.line), channel_id=1, source_target_pairs={{0,7},{1,0},{2,1},{3,2},{4,3},{5,4},{6,5},{7,6},{8,15},{9,8},{10,9... | collective-permute-start | bytes 147464 | tf_op jit(solution)/shard_map/ppermute | solution.py:26
  26.7 7.5 %collective-permute-start.5 = (f32[96,128]{1,0:T(8,128)S(1)}, f32[96,128]{1,0:T(8,128)S(1)}, u32[]{:S(2)}, u32[]{:S(2)}) collective-permute-start(f32[96,128]{1,0:T(8,128)S(1)} %get-tuple-element.32.line), channel_id=1, source_target_pairs={{0,1},{1,2},{2,3},{3,4},{4,5},{5,6},{6,7},{7,0},{8,9},{9,10},{10,1... | collective-permute-start | bytes 147464 | tf_op jit(solution)/shard_map/ppermute | solution.py:26

commit v2 on v1

--- a/solution.py
+++ b/solution.py
@@ -12,7 +12,8 @@
 NB = 8
 NP = 26
 NT = NB * NP
-U = 12
+OWN_U = 12
+GHOST_U = 16
 AHEAD = 2
 LAG = 1
 
@@ -186,6 +187,8 @@
             feat[pl.ds(128 * k + n, nb, stride=16), :] = rows[n] if n < len(rows) else zero
     for p in range(nb):
         j = at[p]
+        if j is None:
+            continue
         fs, ft, fw = (feat[128 * k + 16 * p : 128 * k + 16 * p + 16, :] for k in range(3))
         rb[j] = feat[384 + 16 * p : 384 + 16 * p + 8, :]
         sh, sm, sl = split3(fs)
@@ -267,6 +270,7 @@
         if both:
             mirror_sums(i, j, mirror, wb, cf, acc)
 
+    U = len(cfs)
     trips = (stop - start + U - 1) // U
     for n in range(U - LAG, U):
         cfs[n][...] = jnp.zeros_like(cfs[n])
@@ -298,16 +302,20 @@
     right_prep(lambda c: d[c], NB, range(NB), rb, kb, wb, feat)
     acc[...] = jnp.zeros_like(acc)
     tile_loop(
-        jnp.int32(0), list_ref[3, 0], list_ref, ab, la, rb, kb, wb, bufs[:U], bufs[U:], acc, both=True
+        jnp.int32(0), list_ref[3, 0], list_ref, ab, la, rb, kb, wb, bufs[:OWN_U], bufs[OWN_U:], acc, both=True
     )
 
 
 def ghost_kernel(list_ref, d, ab, la, part, below, line, above, out, acc, rb, kb, wb, feat, *bufs):
     acc[...] = part[...]
-    for ref, lo in ((below, 0), (line, 6), (above, 12)):
-        right_prep(lambda c: ref[pl.ds(c, 6, stride=16), :], 6, range(lo, lo + 6), rb, kb, wb, feat)
+    for ref, at in (
+        (below, (0, 1, 2, 3, 4, 5)),
+        (line, (6, 7, None, None, 10, 11)),
+        (above, (12, 13, 14, 15, 16, 17)),
+    ):
+        right_prep(lambda c: ref[pl.ds(c, 6, stride=16), :], 6, at, rb, kb, wb, feat)
     tile_loop(
-        list_ref[3, 0], list_ref[4, 0], list_ref, ab, la, rb, kb, wb, bufs[:U], bufs[U:], acc, NB
+        list_ref[3, 0], list_ref[4, 0], list_ref, ab, la, rb, kb, wb, bufs[:GHOST_U], bufs[GHOST_U:], acc, NB
     )
     finish(d, acc, out)
 
@@ -375,7 +383,10 @@
     )(*args)
 
 
-WORK = [pltpu.VMEM((1024, 128), bf16)] * U + [pltpu.VMEM((128, 256), f32)] * U
+def work(n):
+    return [pltpu.VMEM((1024, 128), bf16)] * n + [pltpu.VMEM((128, 256), f32)] * n
+
+
 FEAT = pltpu.VMEM((512, 128), f32)
 SUMS = pltpu.VMEM((4 * NB * 16, 128), f32)
 
@@ -394,7 +405,7 @@
         own_kernel,
         [(order, "smem"), (drifted, "vmem")],
         (pltpu.VMEM((NB, 5, 128, 128), f32), pltpu.VMEM((NB, 128, 128), bf16), SUMS),
-        right_refs(NB) + WORK,
+        right_refs(NB) + work(OWN_U),
     )
 
 
@@ -404,7 +415,7 @@
         ghost_kernel,
         [(order, "smem")] + [(x, "vmem") for x in (drifted, ab, la, part, below, line, above)],
         (jax.ShapeDtypeStruct((13, NB, 128), f32),),
-        [SUMS] + right_refs(18) + WORK,
+        [SUMS] + right_refs(18) + work(GHOST_U),
     )
     return out
 
@@ -425,7 +436,6 @@
         (pltpu.SMEM((8, 256), i32),),
         [pltpu.VMEM((8, 256), i32), pltpu.SemaphoreType.DMA(())],
     )
-    order, past, next_slots = lax.optimization_barrier((order, past, next_slots))
     keep, ship, lent, lent_next = kernel_call(
         sort_kernel,
         [(x, "vmem") for x in (mine, past, slots, next_slots)],
@@ -434,6 +444,7 @@
     far = passed_along(lent_next, "gx", 2)
     came = passed_along(ship, "gx", 1)
     fore = passed_along(lent, "gx", -1)
+    order, far, came, fore = lax.optimization_barrier((order, far, came, fore))
     drifted, line = kernel_call(
         join_kernel,
         [(x, "vmem") for x in (keep, came, far, fore, lent_next, slots)],

time: 42.5 us -> 42.7 us (level)
  transfers between devices with their start and end apart: 7 -> 7, of which waited for: 2 -> 3; matrix products, arithmetic and copies ran while one was open for 0% -> 0% of each run, Pallas kernels for 19% -> 19%
where the time goes in v2:
time: 42.7 us; the launch traced here: 42.5 us
  starting transfers between devices  18 us (42%)
  Pallas kernels  17.4 us (41%)
  waiting for transfers between devices  6.44 us (15%)
  between operations  0.7 us (2%)
    ppermute x7, starting transfers between devices, passed_along(): return lax.ppermute(x, axis, [(i, (i + by) % peers) for i in range(peers)])  18 us
    pallas_call x6, Pallas kernels, kernel_call(): pl.pallas_call(body, out_shape=outs, in_specs=[SM if space in ('smem', 's...  17.4 us
    ppermute x7, waiting for transfers between devices, passed_along(): return lax.ppermute(x, axis, [(i, (i + by) % peers) for i in range(peers)])  6.44 us
  transfers between devices with their start and end apart: 7, of which 3 were waited for; matrix products, arithmetic and copies ran while one was open for 0% of the time, Pallas kernels for 19%

profile of v2, /device:TPU:1, one launch (start us, length us, event | category | flops | bytes accessed | tf_op | source)
XLA Modules:
  0.0 42.5 jit_solution(3865133169693089108)
XLA Ops:
  0.0 0.8 %shard_map.56 = (f32[14,8,128]{2,1,0:T(8,128)S(1)}, f32[8,128]{1,0:T(8,128)S(1)}) custom-call(s32[1,8]{1,0:T(1,128)} %home_ref.1, s32[1,2]{1,0:T(1,128)} %lent_ref.1, f32[13,8,128]{2,1,0:T(8,128)} %bitcast.7), custom_call_target="tpu_custom_call" | custom-call | tf_op jit(solution)/shard_map/pallas_call | solution.py:374
  0.8 3.9 %collective-permute-start = (f32[14,8,128]{2,1,0:T(8,128)S(1)}, f32[14,8,128]{2,1,0:T(8,128)S(1)}, u32[]{:S(2)}, u32[]{:S(2)}) collective-permute-start(f32[14,8,128]{2,1,0:T(8,128)S(1)} %get-tuple-element.20.mine), channel_id=1, source_target_pairs={{0,16},{8,24},{16,32},{24,40},{32,48},{40,56},{48,64},{56,72},{64,... | collective-permute-start | bytes 172040 | tf_op jit(solution)/shard_map/ppermute | solution.py:27
  4.7 4.9 %collective-permute-start.1 = (f32[8,128]{1,0:T(8,128)S(1)}, f32[8,128]{1,0:T(8,128)S(1)}, u32[]{:S(2)}, u32[]{:S(2)}) collective-permute-start(f32[8,128]{1,0:T(8,128)S(1)} %get-tuple-element.21.slots), channel_id=1, source_target_pairs={{0,248},{8,0},{16,8},{24,16},{32,24},{40,32},{48,40},{56,48},{64,5... | collective-permute-start | bytes 12296 | tf_op jit(solution)/shard_map/ppermute | solution.py:27
  9.6 0.8 %collective-permute-done.1.next_slots = f32[8,128]{1,0:T(8,128)S(1)} collective-permute-done((f32[8,128]{1,0:T(8,128)S(1)}, f32[8,128]{1,0:T(8,128)S(1)}, u32[]{:S(2)}, u32[]{:S(2)}) %collective-permute-start.1) | collective-permute-done | bytes 4128 | tf_op jit(solution)/shard_map/ppermute | solution.py:27
  10.3 1.3 %collective-permute-done.past = f32[14,8,128]{2,1,0:T(8,128)S(1)} collective-permute-done((f32[14,8,128]{2,1,0:T(8,128)S(1)}, f32[14,8,128]{2,1,0:T(8,128)S(1)}, u32[]{:S(2)}, u32[]{:S(2)}) %collective-permute-start) | collective-permute-done | bytes 57376 | tf_op jit(solution)/shard_map/ppermute | solution.py:27
  11.6 0.2 shard_map.57
  11.8 1.7 %collective-permute-start.3 = (f32[136,128]{1,0:T(8,128)S(1)}, f32[136,128]{1,0:T(8,128)S(1)}, u32[]{:S(2)}, u32[]{:S(2)}) collective-permute-start(f32[136,128]{1,0:T(8,128)S(1)} %get-tuple-element.23), channel_id=1, source_target_pairs={{0,8},{8,16},{16,24},{24,32},{32,40},{40,48},{48,56},{56,64},{64,7... | collective-permute-start | bytes 208904 | tf_op jit(solution)/shard_map/ppermute | solution.py:27
  13.5 3.2 %collective-permute-start.4 = (f32[32,128]{1,0:T(8,128)S(1)}, f32[32,128]{1,0:T(8,128)S(1)}, u32[]{:S(2)}, u32[]{:S(2)}) collective-permute-start(f32[32,128]{1,0:T(8,128)S(1)} %get-tuple-element.24), channel_id=1, source_target_pairs={{0,248},{8,0},{16,8},{24,16},{32,24},{40,32},{48,40},{56,48},{64,5... | collective-permute-start | bytes 49160 | tf_op jit(solution)/shard_map/ppermute | solution.py:27
  16.7 0.0 collective-permute-start.2
  17.3 1.7 %shard_map.55.list_ref = s32[8,256]{1,0:T(8,128)S(4)} custom-call(s32[1,1]{1,0:T(1,128)S(6)} %copy.7.count_ref, s32[2,256]{1,0:T(2,128)} %bitcast.8), custom_call_target="tpu_custom_call" | custom-call | tf_op jit(solution)/shard_map/pallas_call | solution.py:374
  19.1 0.0 collective-permute-done.4.fore
  19.1 4.4 %collective-permute-done.2.far = f32[32,128]{1,0:T(8,128)S(1)} collective-permute-done((f32[32,128]{1,0:T(8,128)S(1)}, f32[32,128]{1,0:T(8,128)S(1)}, u32[]{:S(2)}, u32[]{:S(2)}) %collective-permute-start.2) | collective-permute-done | bytes 16416 | tf_op jit(solution)/shard_map/ppermute | solution.py:27
  23.5 0.0 collective-permute-done.3.came
  23.5 3.2 %collective-permute-start.6 = (f32[96,128]{1,0:T(8,128)S(1)}, f32[96,128]{1,0:T(8,128)S(1)}, u32[]{:S(2)}, u32[]{:S(2)}) collective-permute-start(f32[96,128]{1,0:T(8,128)S(1)} %get-tuple-element.34.line), channel_id=1, source_target_pairs={{0,7},{1,0},{2,1},{3,2},{4,3},{5,4},{6,5},{7,6},{8,15},{9,8},{10,9... | collective-permute-start | bytes 147464 | tf_op jit(solution)/shard_map/ppermute | solution.py:27
  26.7 1.2 %collective-permute-start.5 = (f32[96,128]{1,0:T(8,128)S(1)}, f32[96,128]{1,0:T(8,128)S(1)}, u32[]{:S(2)}, u32[]{:S(2)}) collective-permute-start(f32[96,128]{1,0:T(8,128)S(1)} %get-tuple-element.34.line), channel_id=1, source_target_pairs={{0,1},{1,2},{2,3},{3,4},{4,5},{5,6},{6,7},{7,0},{8,9},{9,10},{10,1... | collective-permute-start | bytes 147464 | tf_op jit(solution)/shard_map/ppermute | solution.py:27
  27.9 6.3 %shard_map.59 = (f32[8,5,128,128]{3,2,1,0:T(8,128)S(1)}, bf16[8,128,128]{2,1,0:T(8,128)(2,1)S(1)}, f32[512,128]{1,0:T(8,128)S(1)}) custom-call(s32[8,256]{1,0:T(8,128)S(4)} %shard_map.55.list_ref, f32[13,8,128]{2,1,0:T(8,128)S(1)} %get-tuple-element.30.d), custom_call_target="tpu_custom_call" | custom-call | tf_op jit(solution)/shard_map/pallas_call | solution.py:374
  34.2 0.0 collective-permute-done.6.above
  34.2 0.0 collective-permute-done.5.below
  34.3 8.3 %shard_map.60 = f32[13,8,128]{2,1,0:T(8,128)} custom-call(s32[8,256]{1,0:T(8,128)S(4)} %shard_map.55.list_ref, f32[13,8,128]{2,1,0:T(8,128)S(1)} %get-tuple-element.30.d, f32[8,5,128,128]{3,2,1,0:T(8,128)S(1)} %get-tuple-element.31.ab, bf16[8,128,128]{2,1,0:T(8,128)(2,1)S(1)} %get-tuple-element.32.la, f32[512,128]{1,0:T(8,128)S(1)} %get-tuple-element.33.part, ...), custom_call_target="tpu_custom_call" | custom-call | tf_op jit(solution)/shard_map/pallas_call | solution.py:374
  (1 shorter events, 0.0 us)
Async XLA Ops:
  0.8 10.8 %collective-permute-start = (f32[14,8,128]{2,1,0:T(8,128)S(1)}, f32[14,8,128]{2,1,0:T(8,128)S(1)}, u32[]{:S(2)}, u32[]{:S(2)}) collective-permute-start(f32[14,8,128]{2,1,0:T(8,128)S(1)} %get-tuple-element.20.mine), channel_id=1, source_target_pairs={{0,16},{8,24},{16,32},{24,40},{32,48},{40,56},{48,64},{56,72},{64,... | collective-permute-start | bytes 172040 | tf_op jit(solution)/shard_map/ppermute | solution.py:27
  4.7 5.6 %collective-permute-start.1 = (f32[8,128]{1,0:T(8,128)S(1)}, f32[8,128]{1,0:T(8,128)S(1)}, u32[]{:S(2)}, u32[]{:S(2)}) collective-permute-start(f32[8,128]{1,0:T(8,128)S(1)} %get-tuple-element.21.slots), channel_id=1, source_target_pairs={{0,248},{8,0},{16,8},{24,16},{32,24},{40,32},{48,40},{56,48},{64,5... | collective-permute-start | bytes 12296 | tf_op jit(solution)/shard_map/ppermute | solution.py:27
  11.8 11.7 %collective-permute-start.3 = (f32[136,128]{1,0:T(8,128)S(1)}, f32[136,128]{1,0:T(8,128)S(1)}, u32[]{:S(2)}, u32[]{:S(2)}) collective-permute-start(f32[136,128]{1,0:T(8,128)S(1)} %get-tuple-element.23), channel_id=1, source_target_pairs={{0,8},{8,16},{16,24},{24,32},{32,40},{40,48},{48,56},{56,64},{64,7... | collective-permute-start | bytes 208904 | tf_op jit(solution)/shard_map/ppermute | solution.py:27
  13.5 5.6 %collective-permute-start.4 = (f32[32,128]{1,0:T(8,128)S(1)}, f32[32,128]{1,0:T(8,128)S(1)}, u32[]{:S(2)}, u32[]{:S(2)}) collective-permute-start(f32[32,128]{1,0:T(8,128)S(1)} %get-tuple-element.24), channel_id=1, source_target_pairs={{0,248},{8,0},{16,8},{24,16},{32,24},{40,32},{48,40},{56,48},{64,5... | collective-permute-start | bytes 49160 | tf_op jit(solution)/shard_map/ppermute | solution.py:27
  16.7 6.8 %collective-permute-start.2 = (f32[32,128]{1,0:T(8,128)S(1)}, f32[32,128]{1,0:T(8,128)S(1)}, u32[]{:S(2)}, u32[]{:S(2)}) collective-permute-start(f32[32,128]{1,0:T(8,128)S(1)} %get-tuple-element.22.lent_next), channel_id=1, source_target_pairs={{0,16},{8,24},{16,32},{24,40},{32,48},{40,56},{48,64},{56,72},{64,... | collective-permute-start | bytes 49160 | tf_op jit(solution)/shard_map/ppermute | solution.py:27
  23.5 10.7 %collective-permute-start.6 = (f32[96,128]{1,0:T(8,128)S(1)}, f32[96,128]{1,0:T(8,128)S(1)}, u32[]{:S(2)}, u32[]{:S(2)}) collective-permute-start(f32[96,128]{1,0:T(8,128)S(1)} %get-tuple-element.34.line), channel_id=1, source_target_pairs={{0,7},{1,0},{2,1},{3,2},{4,3},{5,4},{6,5},{7,6},{8,15},{9,8},{10,9... | collective-permute-start | bytes 147464 | tf_op jit(solution)/shard_map/ppermute | solution.py:27
  26.7 7.5 %collective-permute-start.5 = (f32[96,128]{1,0:T(8,128)S(1)}, f32[96,128]{1,0:T(8,128)S(1)}, u32[]{:S(2)}, u32[]{:S(2)}) collective-permute-start(f32[96,128]{1,0:T(8,128)S(1)} %get-tuple-element.34.line), channel_id=1, source_target_pairs={{0,1},{1,2},{2,3},{3,4},{4,5},{5,6},{6,7},{7,0},{8,9},{9,10},{10,1... | collective-permute-start | bytes 147464 | tf_op jit(solution)/shard_map/ppermute | solution.py:27
